TPU v7x, 32 devices: a whole 2x2x4 slice. The times are simulated.
32 devices in a mesh: gx: 4 (over x, core), gy: 8 (over z, y).
Axes of the slice: x: 2, y: 2, z: 4, core: 2. Of those that a mesh axis runs over, the one named last changes fastest.
Arguments:
- field: float32 [12, 64, 64, 128], P(None, 'gx', 'gy'), may hold values from -16 to 16
- diffusion: float32 [12], replicated, may hold values from 0.02 to 0.15
- prefactor: float32 [12], replicated, may hold values from 0.05 to 0.3
- activation: float32 [12], replicated, may hold values from 0.5 to 2
- mixing: float32 [12, 12], replicated, may hold values from -1.75 to 1.75
- basis_x: float32 [64, 64], P('gx'), may hold values from -1 to 1, as said below
- basis_y: float32 [64, 64], P('gy'), may hold values from -1 to 1, as said below
- basis_z: float32 [128, 32], replicated, may hold values from -1 to 1, as said below
- basis_v: float32 [12, 6], replicated, may hold values from -1 to 1, as said below
Outputs:
- state: float32 [12, 64, 64, 128], P(None, 'gx', 'gy')
- recon: float32 [12, 64, 64, 128], P(None, 'gx', 'gy')
- residual: float32 [12], replicated
Inputs may be any that keep to these rules, and one draw needn't show every extreme that they name: `basis_x`: its 64 columns are mutually orthogonal, each of norm between 0.5 and 1. `basis_y`: its 64 columns are orthonormal. `basis_z`: its 32 columns are orthonormal. `basis_v`: its 6 columns are orthonormal.
All inputs are finite; a program needn't handle non-finite values.
Results may differ from a plain program's by a relative error of at most 0.00013.
Values sent between devices are 32-bit elements; how exact they have to be, the bound alone decides.
No kernel may reach another device: no remote copies, remote signals or barrier semaphores. Data moves between devices by JAX's collectives and lax.ppermute only.
A program may use at most 64 MiB of HBM per device.

v0:
```python
import jax
import jax.numpy as jnp
from jax import lax
from jax.sharding import PartitionSpec as P

HIGH = lax.Precision.HIGHEST


def padded_2(array, sides, width):
    for axis, dim in sides:
        peers, length = (lax.axis_size(axis), array.shape[dim])
        up = [(i, (i + 1) % peers) for i in range(peers - 1)]
        down = [(j, i) for i, j in up]
        last = lax.slice_in_dim(array, length - width, length, axis=dim)
        first = lax.slice_in_dim(array, 0, width, axis=dim)
        before = lax.ppermute(last, axis, up)
        after = lax.ppermute(first, axis, down)
        array = jnp.concatenate([before, array, after], axis=dim)
    return array


def lap_core(padded):
    centre = padded[:, 1:-1, 1:-1, 1:-1]
    summed = padded[:, 2:, 1:-1, 1:-1] + padded[:, :-2, 1:-1, 1:-1]
    summed = summed + padded[:, 1:-1, 2:, 1:-1] + padded[:, 1:-1, :-2, 1:-1]
    summed = summed + padded[:, 1:-1, 1:-1, 2:] + padded[:, 1:-1, 1:-1, :-2]
    return summed - 6.0 * centre


def reaction(centre, coeffs):
    diffusion, prefactor, activation, mixing = coeffs
    temper = 1.5 + jnp.tanh(centre[0])
    rate_terms = (
        prefactor[:, None, None, None]
        * jnp.exp(-activation[:, None, None, None] / temper[None])
        * centre
    )
    return jnp.einsum("vw,wxyz->vxyz", mixing, rate_terms, precision=HIGH)


def tendency(rimmed, centre, coeffs):
    padded = jnp.pad(rimmed, ((0, 0), (0, 0), (0, 0), (1, 1)))
    return coeffs[0][:, None, None, None] * lap_core(padded) + reaction(centre, coeffs)


def inside_mask(rows_x, rows_y):
    pos_x = lax.axis_index("gx") * rows_x + jnp.arange(rows_x + 2) - 1
    pos_y = lax.axis_index("gy") * rows_y + jnp.arange(rows_y + 2) - 1
    in_x = (pos_x >= 0) & (pos_x < rows_x * lax.axis_size("gx"))
    in_y = (pos_y >= 0) & (pos_y < rows_y * lax.axis_size("gy"))
    return in_x[:, None] & in_y[None, :]


def step_deep(state, coeffs, inside):
    wide = padded_2(state, (("gx", 1), ("gy", 2)), 2)
    centre = wide[:, 1:-1, 1:-1]
    section_wide = centre + tendency(wide, centre, coeffs)
    section_wide = jnp.where(inside[None, :, :, None], section_wide, 0.0)
    section = section_wide[:, 1:-1, 1:-1]
    return 0.5 * (state + section + tendency(section_wide, section, coeffs))


def on_device(field, diffusion, prefactor, activation, mixing, basis_x, basis_y, basis_z, basis_v):
    coeffs = (diffusion, prefactor, activation, mixing)
    rows_x = field.shape[1]
    rows_y = field.shape[2]
    state = field
    inside = inside_mask(rows_x, rows_y)
    state = step_deep(state, coeffs, inside)
    rank_z = basis_z.shape[1]
    rank_v = basis_v.shape[1]
    width = rank_z * rank_v
    proj_z = jnp.einsum("vxyz,zr->vxyr", state, basis_z, precision=HIGH)
    packed = jnp.einsum("vxyr,vs->xyrs", proj_z, basis_v, precision=HIGH)
    packed = packed.reshape(rows_x, rows_y, width)
    columns = basis_x
    part_x = lax.psum_scatter(
        jnp.einsum("xa,xyk->ayk", columns, packed, precision=HIGH),
        "gx",
        scatter_dimension=0,
        tiled=True,
    )
    core_block = jnp.einsum("ayk,yb->abk", part_x, basis_y, precision=HIGH)
    core_block = lax.psum(core_block, "gy")
    mixed_y = jnp.einsum("abk,yb->ayk", core_block, basis_y, precision=HIGH)
    columns = basis_x
    decoded = jnp.einsum(
        "xa,ayk->xyk", columns, lax.all_gather(mixed_y, "gx", axis=0, tiled=True), precision=HIGH
    )
    decoded = decoded.reshape(rows_x, rows_y, rank_z, rank_v)
    back_v = jnp.einsum("xyrs,vs->vxyr", decoded, basis_v, precision=HIGH)
    recon = jnp.einsum("vxyr,zr->vxyz", back_v, basis_z, precision=HIGH)
    error = state - recon
    miss_local = jnp.sum(error * error, axis=(1, 2, 3))
    mass_local = jnp.sum(state * state, axis=(1, 2, 3))
    miss, mass = lax.psum((miss_local, mass_local), ("gx", "gy"))
    residual = jnp.sqrt(miss / (mass + 1e-06))
    return (state, recon, residual)


def solution(mesh):
    return jax.shard_map(
        on_device,
        mesh=mesh,
        in_specs=(
            P(None, "gx", "gy", None),
            P(),
            P(),
            P(),
            P(),
            P("gx", None),
            P("gy", None),
            P(),
            P(),
        ),
        out_specs=(P(None, "gx", "gy", None), P(None, "gx", "gy", None), P()),
        check_vma=False,
    )
```

profile of v0, /device:TPU:0, one launch (start us, length us, event | category | flops | bytes accessed | tf_op | source)
XLA Modules:
  0.0 209.1 jit_solution(7740615977400366910)
XLA Ops:
  7.2 1.0 fusion.57
  8.3 2.4 %collective-permute-start = (f32[12,2,8,128]{3,0,2,1:T(8,128)S(1)}, f32[12,2,8,128]{3,0,2,1:T(8,128)S(1)}, u32[]{:S(2)}, u32[]{:S(2)}) collective-permute-start(f32[12,2,8,128]{3,0,2,1:T(8,128)S(1)} %copy.76), channel_id=1, source_target_pairs={{0,8},{8,16},{16,24},{1,9},{9,17},{17,25},{2,10},{10,18},{18,26},{... | collective-permute-start | bytes 294920 | tf_op jit(solution)/shard_map/ppermute | solution.py:16
  10.8 1.3 collective-permute-start.1
  12.6 3.5 %collective-permute-done.1 = f32[12,2,8,128]{3,0,2,1:T(8,128)S(1)} collective-permute-done((f32[12,2,8,128]{3,0,2,1:T(8,128)S(1)}, f32[12,2,8,128]{3,0,2,1:T(8,128)S(1)}, u32[]{:S(2)}, u32[]{:S(2)}) %collective-permute-start.1) | collective-permute-done | bytes 98336 | tf_op jit(solution)/shard_map/ppermute | solution.py:17
  16.2 3.4 %collective-permute-start.2 = (f32[12,20,2,128]{3,0,2,1:T(8,128)S(1)}, f32[12,20,2,128]{3,0,2,1:T(8,128)S(1)}, u32[]{:S(2)}, u32[]{:S(2)}) collective-permute-start(f32[12,20,2,128]{3,0,2,1:T(8,128)S(1)} %get-tuple-element.19), channel_id=1, source_target_pairs={{0,1},{1,2},{2,3},{3,4},{4,5},{5,6},{6,7},{8,9},{9,10},{10,11},{11... | collective-permute-start | bytes 737288 | tf_op jit(solution)/shard_map/ppermute | solution.py:16
  19.6 1.3 collective-permute-start.3
  21.0 4.2 %collective-permute-done.2 = f32[12,20,2,128]{3,0,2,1:T(8,128)S(1)} collective-permute-done((f32[12,20,2,128]{3,0,2,1:T(8,128)S(1)}, f32[12,20,2,128]{3,0,2,1:T(8,128)S(1)}, u32[]{:S(2)}, u32[]{:S(2)}) %collective-permute-start.2) | collective-permute-done | bytes 245792 | tf_op jit(solution)/shard_map/ppermute | solution.py:16
  25.2 4.6 %collective-permute-done.3 = f32[12,20,2,128]{3,0,2,1:T(8,128)S(1)} collective-permute-done((f32[12,20,2,128]{3,0,2,1:T(8,128)S(1)}, f32[12,20,2,128]{3,0,2,1:T(8,128)S(1)}, u32[]{:S(2)}, u32[]{:S(2)}) %collective-permute-start.3) | collective-permute-done | bytes 245792 | tf_op jit(solution)/shard_map/ppermute | solution.py:17
  30.1 2.3 %fusion.8 = f32[12,18,10,128]{3,0,2,1:T(8,128)S(1)} fusion(f32[12,20,12,128]{3,0,2,1:T(8,128)S(1)} %pad_maximum_fusion, f32[12,20,8,128]{3,0,2,1:T(8,128)S(1)} %constant_dynamic-update-slice_fusion, f32[12,20,2,128]{3,0,2,1:T(8,128)S(1)} %collective-permute-done.2, f32[12,20,2,128]{3,0,2,1:T(8,128)S(1)} %collective-permute-done.3, ...), kind=kOutput, calls=%fused_computation.14 | convolution fusion | flops 44236800 | bytes 11096576 | tf_op jit(solution)/shard_map/vw,wxyz->vxyz/dot_general | solution.py:38
  32.6 2.2 %fusion.23 = f32[12,16,8,128]{3,0,2,1:T(8,128)S(1)} fusion(f32[12,18,10,128]{3,0,2,1:T(8,128)S(1)} %fusion.8, f32[16,8,128]{2,1,0:T(8,128)S(1)} %bitcast.62, f32[12]{0:T(128)S(1)} %neg.5, f32[12]{0:T(128)S(1)} %copy-done.8, f32[12]{0:T(128)S(1)} %copy-done.9, f32[12,16,8,128]{3,2,1,0:T(8,128)S(1)} %copy-done.2, f32[12,12]{1,0:T(8,128)S(1)} %copy-done.6), kind=kOutput, calls=%fused_computation.37 | convolution fusion | flops 31260672 | bytes 9414144 | tf_op jit(solution)/shard_map/vw,wxyz->vxyz/dot_general | solution.py:38
  34.8 1.0 fusion.44
  35.8 0.7 fusion.51
  37.1 1.7 convolution_bitcast_fusion.3
  38.7 1.1 copy.51
  39.9 27.8 %reduce-scatter.2.cloned.1.call-done = f32[16,8,192]{2,1,0:T(8,128)} async-done(((f32[64,8,192]{2,1,0:T(8,128)}), f32[16,8,192]{2,1,0:T(8,128)}) %reduce-scatter.2.cloned.1.call-update) | async-done | bytes 98320 | tf_op jit(solution)/shard_map/reduce_scatter | solution.py:77
  67.7 2.9 %convolution_bitcast_fusion.1 = f32[16,64,192]{2,1,0:T(8,128)} fusion(f32[16,8,192]{2,1,0:T(8,128)} %reduce-scatter.2.cloned.1.call-done, f32[8,64]{1,0:T(8,128)S(1)} %copy-done.4), kind=kOutput, calls=%fused_computation.23 | convolution fusion | flops 18874368 | bytes 886784 | tf_op jit(solution)/shard_map/ayk,yb->abk/dot_general | solution.py:83
  70.6 1.1 copy.57
  71.7 77.8 %all-reduce.5.cloned.1.call-done = f32[16,64,192]{2,1,0:T(8,128)} async-done(((f32[16,64,192]{2,1,0:T(8,128)}), f32[16,64,192]{2,1,0:T(8,128)}) %all-reduce.5.cloned.1.call-update) | async-done | bytes 786448 | tf_op jit(solution)/shard_map/psum | solution.py:84
  149.5 1.9 convolution_bitcast_fusion.5
  151.3 7.3 %all_gather.3 = f32[64,8,192]{2,1,0:T(8,128)S(1)} all-gather(f32[16,8,192]{2,1,0:T(8,128)S(1)} %convolution_bitcast_fusion.5), channel_id=1, replica_groups=mesh['gx'=4,'gy'=8] {'gx'}, dimensions={0}, use_global_device_ids=true | all-gather | bytes 491520 | tf_op jit(solution)/shard_map/all_gather | solution.py:88
  160.1 1.0 convolution_bitcast_fusion
  161.2 0.9 fusion.31
  162.1 0.7 multiply_reduce_fusion
  162.8 38.9 %all-reduce.2 = (f32[12]{0:T(128)S(1)}, f32[12]{0:T(128)S(1)}) all-reduce(f32[12]{0:T(128)S(1)} %get-tuple-element.16, f32[12]{0:T(128)S(1)} %get-tuple-element.15), channel_id=1, replica_groups=mesh['gx'=4,'gy'=8] {'gx','gy'}, use_global_device_ids=true, to_apply=%region_3.4 | all-reduce | flops 24 | bytes 192 | tf_op jit(solution)/shard_map/psum | solution.py:96
  (44 shorter events, 3.7 us)
Async XLA Ops:
  7.2 27.6 %copy-start = (f32[128,32]{0,1:T(8,128)S(1)}, f32[128,32]{0,1:T(8,128)}, u32[]{:S(2)}) copy-start(f32[128,32]{0,1:T(8,128)} %param.16) | copy-start | bytes 49156
  7.2 4.9 %copy-start.2 = (f32[12,16,8,128]{3,2,1,0:T(8,128)S(1)}, f32[12,16,8,128]{3,2,1,0:T(8,128)}, u32[]{:S(2)}) copy-start(f32[12,16,8,128]{3,2,1,0:T(8,128)} %param.9) | copy-start | bytes 2359300
  7.2 60.5 %reduce-scatter.2.cloned.1.call-start = ((), (), s32[]{:S(2)}) async-start(), calls=%async_computation.1 | async-start | bytes 655360 | tf_op jit(solution)/shard_map/reduce_scatter | solution.py:77
  8.3 3.8 %collective-permute-start = (f32[12,2,8,128]{3,0,2,1:T(8,128)S(1)}, f32[12,2,8,128]{3,0,2,1:T(8,128)S(1)}, u32[]{:S(2)}, u32[]{:S(2)}) collective-permute-start(f32[12,2,8,128]{3,0,2,1:T(8,128)S(1)} %copy.76), channel_id=1, source_target_pairs={{0,8},{8,16},{16,24},{1,9},{9,17},{17,25},{2,10},{10,18},{18,26},{... | collective-permute-start | bytes 294920 | tf_op jit(solution)/shard_map/ppermute | solution.py:16
  10.8 5.3 %collective-permute-start.1 = (f32[12,2,8,128]{3,0,2,1:T(8,128)S(1)}, f32[12,2,8,128]{3,0,2,1:T(8,128)S(1)}, u32[]{:S(2)}, u32[]{:S(2)}) collective-permute-start(f32[12,2,8,128]{3,0,2,1:T(8,128)S(1)} %copy.77), channel_id=1, source_target_pairs={{8,0},{16,8},{24,16},{9,1},{17,9},{25,17},{10,2},{18,10},{26,18},{... | collective-permute-start | bytes 294920 | tf_op jit(solution)/shard_map/ppermute | solution.py:17
  12.1 8.8 %copy-start.7 = (f32[12]{0:T(128)S(1)}, f32[12]{0:T(128)}, u32[]{:S(2)}) copy-start(f32[12]{0:T(128)} %param.12) | copy-start | bytes 148
  16.2 9.0 %collective-permute-start.2 = (f32[12,20,2,128]{3,0,2,1:T(8,128)S(1)}, f32[12,20,2,128]{3,0,2,1:T(8,128)S(1)}, u32[]{:S(2)}, u32[]{:S(2)}) collective-permute-start(f32[12,20,2,128]{3,0,2,1:T(8,128)S(1)} %get-tuple-element.19), channel_id=1, source_target_pairs={{0,1},{1,2},{2,3},{3,4},{4,5},{5,6},{6,7},{8,9},{9,10},{10,11},{11... | collective-permute-start | bytes 737288 | tf_op jit(solution)/shard_map/ppermute | solution.py:16
  19.6 10.2 %collective-permute-start.3 = (f32[12,20,2,128]{3,0,2,1:T(8,128)S(1)}, f32[12,20,2,128]{3,0,2,1:T(8,128)S(1)}, u32[]{:S(2)}, u32[]{:S(2)}) collective-permute-start(f32[12,20,2,128]{3,0,2,1:T(8,128)S(1)} %get-tuple-element.20), channel_id=1, source_target_pairs={{1,0},{2,1},{3,2},{4,3},{5,4},{6,5},{7,6},{9,8},{10,9},{11,10},{12... | collective-permute-start | bytes 737288 | tf_op jit(solution)/shard_map/ppermute | solution.py:17
  21.0 9.1 %copy-start.6 = (f32[12,12]{1,0:T(8,128)S(1)}, f32[12,12]{1,0:T(8,128)}, u32[]{:S(2)}) copy-start(f32[12,12]{1,0:T(8,128)} %param.13) | copy-start | bytes 1732
  21.0 9.1 %copy-start.8 = (f32[12]{0:T(128)S(1)}, f32[12]{0:T(128)}, u32[]{:S(2)}) copy-start(f32[12]{0:T(128)} %param.11) | copy-start | bytes 148
  21.0 9.1 %copy-start.9 = (f32[12]{0:T(128)S(1)}, f32[12]{0:T(128)}, u32[]{:S(2)}) copy-start(f32[12]{0:T(128)} %param.10) | copy-start | bytes 148
  34.8 1.0 copy-start.5
  35.8 1.3 copy-start.3
  37.1 30.6 %copy-start.4 = (f32[8,64]{1,0:T(8,128)S(1)}, f32[8,64]{1,0:T(8,128)}, u32[]{:S(2)}) copy-start(f32[8,64]{1,0:T(8,128)} %param.15) | copy-start | bytes 6148
  39.9 109.6 %all-reduce.5.cloned.1.call-start = ((), (), s32[]{:S(2)}) async-start(), calls=%async_computation.2 | async-start | bytes 2097152 | tf_op jit(solution)/shard_map/psum | solution.py:84
  162.1 40.1 %copy-start.1 = (f32[12,16,8,128]{3,2,1,0:T(8,128)}, f32[12,16,8,128]{3,2,1,0:T(8,128)S(1)}, u32[]{:S(2)}) copy-start(f32[12,16,8,128]{3,2,1,0:T(8,128)S(1)} %fusion.31) | copy-start | bytes 2359300
Sparse Core Ops, SparseCore 0:
  40.0 27.6 reduce-scatter.1
  71.2 78.2 all-reduce.4
where the time goes:
time: 209 us
  waiting for transfers between devices  118 us (56%)
  blocking collectives  46.3 us (22%)
  matrix products  15.1 us (7%)
  between operations  14.4 us (7%)
  starting transfers between devices  8.51 us (4%)
  local copies, waits for them, and re-layouts  5.35 us (3%)
    psum x1, waiting for transfers between devices, on_device(): core_block = lax.psum(core_block, 'gy')  77.8 us
    psum x1, blocking collectives, on_device(): miss, mass = lax.psum((miss_local, mass_local), ('gx', 'gy'))  38.9 us
    reduce_scatter x1, waiting for transfers between devices, on_device(): lax.psum_scatter(jnp.einsum('xa,xyk->ayk', columns, packed, precision=HIG...  27.8 us
    ppermute x2, waiting for transfers between devices, padded_2(): after = lax.ppermute(first, axis, down)  8.07 us
    all_gather x1, blocking collectives, on_device(): lax.all_gather(mixed_y, 'gx', axis=0, tiled=True)  7.32 us
    ppermute x2, starting transfers between devices, padded_2(): before = lax.ppermute(last, axis, up)  5.85 us
    dot_general x2, matrix products, reaction(): return jnp.einsum('vw,wxyz->vxyz', mixing, rate_terms, precision=HIGH)  4.55 us
  transfers between devices with their start and end apart: 6, of which 5 were waited for; matrix products, arithmetic and copies ran while one was open for 1% of the time, Pallas kernels for 0%

commit v1 on v0

--- a/solution.py
+++ b/solution.py
@@ -93,7 +93,7 @@
     error = state - recon
     miss_local = jnp.sum(error * error, axis=(1, 2, 3))
     mass_local = jnp.sum(state * state, axis=(1, 2, 3))
-    miss, mass = lax.psum((miss_local, mass_local), ("gx", "gy"))
+    miss, mass = lax.psum(lax.psum((miss_local, mass_local), "gy"), "gx")
     residual = jnp.sqrt(miss / (mass + 1e-06))
     return (state, recon, residual)
 

time: 209 us -> 196 us (0.938)
  blocking collectives: 46.3 us -> 33 us
    psum x1 -> x2, blocking collectives: 38.9 us -> 25.7 us  [on_device(): miss, mass = lax.psum(lax.psum((miss_local, mass_local), 'gy'), 'gx')]
where the time goes in v1:
time: 196 us
  waiting for transfers between devices  118 us (60%)
  blocking collectives  33 us (17%)
  matrix products  15.1 us (8%)
  between operations  14.4 us (7%)
  starting transfers between devices  8.51 us (4%)
  local copies, waits for them, and re-layouts  5.35 us (3%)
    psum x1, waiting for transfers between devices, on_device(): core_block = lax.psum(core_block, 'gy')  77.8 us
    reduce_scatter x1, waiting for transfers between devices, on_device(): lax.psum_scatter(jnp.einsum('xa,xyk->ayk', columns, packed, precision=HIG...  27.8 us
    psum x2, blocking collectives, on_device(): miss, mass = lax.psum(lax.psum((miss_local, mass_local), 'gy'), 'gx')  25.7 us
    ppermute x2, waiting for transfers between devices, padded_2(): after = lax.ppermute(first, axis, down)  8.07 us
    all_gather x1, blocking collectives, on_device(): lax.all_gather(mixed_y, 'gx', axis=0, tiled=True)  7.32 us
    ppermute x2, starting transfers between devices, padded_2(): before = lax.ppermute(last, axis, up)  5.85 us
    dot_general x2, matrix products, reaction(): return jnp.einsum('vw,wxyz->vxyz', mixing, rate_terms, precision=HIGH)  4.55 us
    ppermute x2, waiting for transfers between devices, padded_2(): before = lax.ppermute(last, axis, up)  4.17 us
  transfers between devices with their start and end apart: 6, of which 5 were waited for; matrix products, arithmetic and copies ran while one was open for 1% of the time, Pallas kernels for 0%

profile of v1, /device:TPU:0, one launch (start us, length us, event | category | flops | bytes accessed | tf_op | source)
XLA Modules:
  0.0 195.8 jit_solution(8393898822845535089)
XLA Ops:
  7.2 1.0 fusion.57
  8.3 2.4 %collective-permute-start = (f32[12,2,8,128]{3,0,2,1:T(8,128)S(1)}, f32[12,2,8,128]{3,0,2,1:T(8,128)S(1)}, u32[]{:S(2)}, u32[]{:S(2)}) collective-permute-start(f32[12,2,8,128]{3,0,2,1:T(8,128)S(1)} %copy.76), channel_id=1, source_target_pairs={{0,8},{8,16},{16,24},{1,9},{9,17},{17,25},{2,10},{10,18},{18,26},{... | collective-permute-start | bytes 294920 | tf_op jit(solution)/shard_map/ppermute | solution.py:16
  10.8 1.3 collective-permute-start.1
  12.6 3.5 %collective-permute-done.1 = f32[12,2,8,128]{3,0,2,1:T(8,128)S(1)} collective-permute-done((f32[12,2,8,128]{3,0,2,1:T(8,128)S(1)}, f32[12,2,8,128]{3,0,2,1:T(8,128)S(1)}, u32[]{:S(2)}, u32[]{:S(2)}) %collective-permute-start.1) | collective-permute-done | bytes 98336 | tf_op jit(solution)/shard_map/ppermute | solution.py:17
  16.2 3.4 %collective-permute-start.2 = (f32[12,20,2,128]{3,0,2,1:T(8,128)S(1)}, f32[12,20,2,128]{3,0,2,1:T(8,128)S(1)}, u32[]{:S(2)}, u32[]{:S(2)}) collective-permute-start(f32[12,20,2,128]{3,0,2,1:T(8,128)S(1)} %get-tuple-element.21), channel_id=1, source_target_pairs={{0,1},{1,2},{2,3},{3,4},{4,5},{5,6},{6,7},{8,9},{9,10},{10,11},{11... | collective-permute-start | bytes 737288 | tf_op jit(solution)/shard_map/ppermute | solution.py:16
  19.6 1.3 collective-permute-start.3
  21.0 4.2 %collective-permute-done.2 = f32[12,20,2,128]{3,0,2,1:T(8,128)S(1)} collective-permute-done((f32[12,20,2,128]{3,0,2,1:T(8,128)S(1)}, f32[12,20,2,128]{3,0,2,1:T(8,128)S(1)}, u32[]{:S(2)}, u32[]{:S(2)}) %collective-permute-start.2) | collective-permute-done | bytes 245792 | tf_op jit(solution)/shard_map/ppermute | solution.py:16
  25.2 4.6 %collective-permute-done.3 = f32[12,20,2,128]{3,0,2,1:T(8,128)S(1)} collective-permute-done((f32[12,20,2,128]{3,0,2,1:T(8,128)S(1)}, f32[12,20,2,128]{3,0,2,1:T(8,128)S(1)}, u32[]{:S(2)}, u32[]{:S(2)}) %collective-permute-start.3) | collective-permute-done | bytes 245792 | tf_op jit(solution)/shard_map/ppermute | solution.py:17
  30.1 2.3 %fusion.8 = f32[12,18,10,128]{3,0,2,1:T(8,128)S(1)} fusion(f32[12,20,12,128]{3,0,2,1:T(8,128)S(1)} %pad_maximum_fusion, f32[12,20,8,128]{3,0,2,1:T(8,128)S(1)} %constant_dynamic-update-slice_fusion, f32[12,20,2,128]{3,0,2,1:T(8,128)S(1)} %collective-permute-done.2, f32[12,20,2,128]{3,0,2,1:T(8,128)S(1)} %collective-permute-done.3, ...), kind=kOutput, calls=%fused_computation.14 | convolution fusion | flops 44236800 | bytes 11096576 | tf_op jit(solution)/shard_map/vw,wxyz->vxyz/dot_general | solution.py:38
  32.6 2.2 %fusion.23 = f32[12,16,8,128]{3,0,2,1:T(8,128)S(1)} fusion(f32[12,18,10,128]{3,0,2,1:T(8,128)S(1)} %fusion.8, f32[16,8,128]{2,1,0:T(8,128)S(1)} %bitcast.62, f32[12]{0:T(128)S(1)} %neg.5, f32[12]{0:T(128)S(1)} %copy-done.8, f32[12]{0:T(128)S(1)} %copy-done.9, f32[12,16,8,128]{3,2,1,0:T(8,128)S(1)} %copy-done.2, f32[12,12]{1,0:T(8,128)S(1)} %copy-done.6), kind=kOutput, calls=%fused_computation.37 | convolution fusion | flops 31260672 | bytes 9414144 | tf_op jit(solution)/shard_map/vw,wxyz->vxyz/dot_general | solution.py:38
  34.8 1.0 fusion.44
  35.8 0.7 fusion.51
  37.1 1.7 convolution_bitcast_fusion.3
  38.7 1.1 copy.51
  39.9 27.8 %reduce-scatter.2.cloned.1.call-done = f32[16,8,192]{2,1,0:T(8,128)} async-done(((f32[64,8,192]{2,1,0:T(8,128)}), f32[16,8,192]{2,1,0:T(8,128)}) %reduce-scatter.2.cloned.1.call-update) | async-done | bytes 98320 | tf_op jit(solution)/shard_map/reduce_scatter | solution.py:77
  67.7 2.9 %convolution_bitcast_fusion.1 = f32[16,64,192]{2,1,0:T(8,128)} fusion(f32[16,8,192]{2,1,0:T(8,128)} %reduce-scatter.2.cloned.1.call-done, f32[8,64]{1,0:T(8,128)S(1)} %copy-done.4), kind=kOutput, calls=%fused_computation.23 | convolution fusion | flops 18874368 | bytes 886784 | tf_op jit(solution)/shard_map/ayk,yb->abk/dot_general | solution.py:83
  70.6 1.1 copy.57
  71.7 77.8 %all-reduce.6.cloned.1.call-done = f32[16,64,192]{2,1,0:T(8,128)} async-done(((f32[16,64,192]{2,1,0:T(8,128)}), f32[16,64,192]{2,1,0:T(8,128)}) %all-reduce.6.cloned.1.call-update) | async-done | bytes 786448 | tf_op jit(solution)/shard_map/psum | solution.py:84
  149.5 1.9 convolution_bitcast_fusion.5
  151.3 7.3 %all_gather.3 = f32[64,8,192]{2,1,0:T(8,128)S(1)} all-gather(f32[16,8,192]{2,1,0:T(8,128)S(1)} %convolution_bitcast_fusion.5), channel_id=1, replica_groups=mesh['gx'=4,'gy'=8] {'gx'}, dimensions={0}, use_global_device_ids=true | all-gather | bytes 491520 | tf_op jit(solution)/shard_map/all_gather | solution.py:88
  160.1 1.0 convolution_bitcast_fusion
  161.2 0.9 fusion.31
  162.8 20.0 %all-reduce.2 = (f32[12]{0:T(128)S(1)}, f32[12]{0:T(128)S(1)}) all-reduce(f32[12]{0:T(128)S(1)} %get-tuple-element.16, f32[12]{0:T(128)S(1)} %get-tuple-element.15), channel_id=1, replica_groups=mesh['gx'=4,'gy'=8] {'gy'}, use_global_device_ids=true, to_apply=%region_3.4 | all-reduce | flops 24 | bytes 192 | tf_op jit(solution)/shard_map/psum | solution.py:96
  182.8 5.6 %all-reduce.3 = (f32[12]{0:T(128)S(1)}, f32[12]{0:T(128)S(1)}) all-reduce(f32[12]{0:T(128)S(1)} %get-tuple-element.17, f32[12]{0:T(128)S(1)} %get-tuple-element.18), channel_id=1, replica_groups=mesh['gx'=4,'gy'=8] {'gx'}, use_global_device_ids=true, to_apply=%region_4.5 | all-reduce | flops 24 | bytes 192 | tf_op jit(solution)/shard_map/psum | solution.py:96
  (45 shorter events, 4.4 us)
Async XLA Ops:
  7.2 27.6 %copy-start = (f32[128,32]{0,1:T(8,128)S(1)}, f32[128,32]{0,1:T(8,128)}, u32[]{:S(2)}) copy-start(f32[128,32]{0,1:T(8,128)} %param.16) | copy-start | bytes 49156
  7.2 4.9 %copy-start.2 = (f32[12,16,8,128]{3,2,1,0:T(8,128)S(1)}, f32[12,16,8,128]{3,2,1,0:T(8,128)}, u32[]{:S(2)}) copy-start(f32[12,16,8,128]{3,2,1,0:T(8,128)} %param.9) | copy-start | bytes 2359300
  7.2 60.5 %reduce-scatter.2.cloned.1.call-start = ((), (), s32[]{:S(2)}) async-start(), calls=%async_computation.1 | async-start | bytes 655360 | tf_op jit(solution)/shard_map/reduce_scatter | solution.py:77
  8.3 3.8 %collective-permute-start = (f32[12,2,8,128]{3,0,2,1:T(8,128)S(1)}, f32[12,2,8,128]{3,0,2,1:T(8,128)S(1)}, u32[]{:S(2)}, u32[]{:S(2)}) collective-permute-start(f32[12,2,8,128]{3,0,2,1:T(8,128)S(1)} %copy.76), channel_id=1, source_target_pairs={{0,8},{8,16},{16,24},{1,9},{9,17},{17,25},{2,10},{10,18},{18,26},{... | collective-permute-start | bytes 294920 | tf_op jit(solution)/shard_map/ppermute | solution.py:16
  10.8 5.3 %collective-permute-start.1 = (f32[12,2,8,128]{3,0,2,1:T(8,128)S(1)}, f32[12,2,8,128]{3,0,2,1:T(8,128)S(1)}, u32[]{:S(2)}, u32[]{:S(2)}) collective-permute-start(f32[12,2,8,128]{3,0,2,1:T(8,128)S(1)} %copy.77), channel_id=1, source_target_pairs={{8,0},{16,8},{24,16},{9,1},{17,9},{25,17},{10,2},{18,10},{26,18},{... | collective-permute-start | bytes 294920 | tf_op jit(solution)/shard_map/ppermute | solution.py:17
  12.1 8.8 %copy-start.7 = (f32[12]{0:T(128)S(1)}, f32[12]{0:T(128)}, u32[]{:S(2)}) copy-start(f32[12]{0:T(128)} %param.12) | copy-start | bytes 148
  16.2 9.0 %collective-permute-start.2 = (f32[12,20,2,128]{3,0,2,1:T(8,128)S(1)}, f32[12,20,2,128]{3,0,2,1:T(8,128)S(1)}, u32[]{:S(2)}, u32[]{:S(2)}) collective-permute-start(f32[12,20,2,128]{3,0,2,1:T(8,128)S(1)} %get-tuple-element.21), channel_id=1, source_target_pairs={{0,1},{1,2},{2,3},{3,4},{4,5},{5,6},{6,7},{8,9},{9,10},{10,11},{11... | collective-permute-start | bytes 737288 | tf_op jit(solution)/shard_map/ppermute | solution.py:16
  19.6 10.2 %collective-permute-start.3 = (f32[12,20,2,128]{3,0,2,1:T(8,128)S(1)}, f32[12,20,2,128]{3,0,2,1:T(8,128)S(1)}, u32[]{:S(2)}, u32[]{:S(2)}) collective-permute-start(f32[12,20,2,128]{3,0,2,1:T(8,128)S(1)} %get-tuple-element.22), channel_id=1, source_target_pairs={{1,0},{2,1},{3,2},{4,3},{5,4},{6,5},{7,6},{9,8},{10,9},{11,10},{12... | collective-permute-start | bytes 737288 | tf_op jit(solution)/shard_map/ppermute | solution.py:17
  21.0 9.1 %copy-start.6 = (f32[12,12]{1,0:T(8,128)S(1)}, f32[12,12]{1,0:T(8,128)}, u32[]{:S(2)}) copy-start(f32[12,12]{1,0:T(8,128)} %param.13) | copy-start | bytes 1732
  21.0 9.1 %copy-start.8 = (f32[12]{0:T(128)S(1)}, f32[12]{0:T(128)}, u32[]{:S(2)}) copy-start(f32[12]{0:T(128)} %param.11) | copy-start | bytes 148
  21.0 9.1 %copy-start.9 = (f32[12]{0:T(128)S(1)}, f32[12]{0:T(128)}, u32[]{:S(2)}) copy-start(f32[12]{0:T(128)} %param.10) | copy-start | bytes 148
  34.8 1.0 copy-start.5
  35.8 1.3 copy-start.3
  37.1 30.6 %copy-start.4 = (f32[8,64]{1,0:T(8,128)S(1)}, f32[8,64]{1,0:T(8,128)}, u32[]{:S(2)}) copy-start(f32[8,64]{1,0:T(8,128)} %param.15) | copy-start | bytes 6148
  39.9 109.6 %all-reduce.6.cloned.1.call-start = ((), (), s32[]{:S(2)}) async-start(), calls=%async_computation.2 | async-start | bytes 2097152 | tf_op jit(solution)/shard_map/psum | solution.py:84
  162.1 26.9 %copy-start.1 = (f32[12,16,8,128]{3,2,1,0:T(8,128)}, f32[12,16,8,128]{3,2,1,0:T(8,128)S(1)}, u32[]{:S(2)}) copy-start(f32[12,16,8,128]{3,2,1,0:T(8,128)S(1)} %fusion.31) | copy-start | bytes 2359300
Sparse Core Ops, SparseCore 0:
  40.0 27.6 reduce-scatter.1
  71.2 78.2 all-reduce.5
